TPU v7x, 32 devices: a whole 2x2x4 slice. The times are simulated.
32 devices in a mesh: dp: 8 (over z, y), tensor: 4 (over x, core).
Axes of the slice: x: 2, y: 2, z: 4, core: 2. Of those that a mesh axis runs over, the one named last changes fastest.
Arguments:
- tokens: bfloat16 [16384, 768], P(('dp', 'tensor')), may hold values from -6 to 6
- cotangent: bfloat16 [16384, 768], P(('dp', 'tensor')), may hold values from -6 to 6
- segment_ids: int32 [8, 2048], P('dp'), may hold values from 0 to 7, never falling along the last dimension, each value on 1 to 512 neighbouring positions
- ln1_gain: bfloat16 [768], P('dp'), may hold values from 0.5 to 1.5
- ln1_bias: bfloat16 [768], P('dp'), may hold values from -3 to 3
- w_query: bfloat16 [768, 768], P('dp', 'tensor'), may hold values from -0.3125 to 0.3125
- query_bias: bfloat16 [768], P('dp'), may hold values from -3 to 3
- w_key: bfloat16 [768, 768], P('dp', 'tensor'), may hold values from -0.3125 to 0.3125
- w_value: bfloat16 [768, 768], P('dp', 'tensor'), may hold values from -0.21875 to 0.21875
- value_bias: bfloat16 [768], P('dp'), may hold values from -3 to 3
- w_out: bfloat16 [768, 768], P('tensor', 'dp'), may hold values from -0.625 to 0.625
- out_bias: bfloat16 [768], P('dp'), may hold values from -3 to 3
- ln2_gain: bfloat16 [768], P('dp'), may hold values from 0.5 to 1.5
- ln2_bias: bfloat16 [768], P('dp'), may hold values from -3 to 3
- w_in: bfloat16 [768, 3072], P('dp', 'tensor'), may hold values from -0.21875 to 0.21875
- in_bias: bfloat16 [3072], P('dp'), may hold values from -3 to 3
- w_back: bfloat16 [3072, 768], P('tensor', 'dp'), may hold values from -0.15625 to 0.15625
- back_bias: bfloat16 [768], P('dp'), may hold values from -3 to 3
Outputs:
- output: bfloat16 [16384, 768], P(('dp', 'tensor'))
- grad_tokens: float32 [16384, 768], P(('dp', 'tensor'))
- grad_ln1_gain: float32 [768], P('dp')
- grad_ln1_bias: float32 [768], P('dp')
- grad_w_query: float32 [768, 768], P('dp', 'tensor')
- grad_query_bias: float32 [768], P('dp')
- grad_w_key: float32 [768, 768], P('dp', 'tensor')
- grad_w_value: float32 [768, 768], P('dp', 'tensor')
- grad_value_bias: float32 [768], P('dp')
- grad_w_out: float32 [768, 768], P('tensor', 'dp')
- grad_out_bias: float32 [768], P('dp')
- grad_ln2_gain: float32 [768], P('dp')
- grad_ln2_bias: float32 [768], P('dp')
- grad_w_in: float32 [768, 3072], P('dp', 'tensor')
- grad_in_bias: float32 [3072], P('dp')
- grad_w_back: float32 [3072, 768], P('tensor', 'dp')
- grad_back_bias: float32 [768], P('dp')
Inputs may be any that keep to these rules, and one draw needn't show every extreme that they name: `segment_ids`: in each sequence the document numbers never fall; every number 0 to 7 appears, on 1 to 512 consecutive patches, and some document has exactly 512.
All inputs are finite; a program needn't handle non-finite values.
Results may differ from a plain program's by a relative error of at most 0.02.
Values may be sent and summed in bfloat16 or wider, within the bound.
A program may use at most 128 MiB of HBM per device.

v0:
```python
import math
import jax
import jax.numpy as jnp
from jax import lax
from jax.sharding import PartitionSpec as P

HEAD_DIM = 64
EPSILON = 1e-12


def layer_norm(values, gain, shift):
    center = values - jnp.mean(values, axis=-1, keepdims=True)
    spread = jnp.mean(center * center, axis=-1, keepdims=True)
    return center * lax.rsqrt(spread + EPSILON) * gain + shift


def gelu_exact(values):
    return jax.nn.gelu(values, approximate=False)


def contract_rows(left, right):
    return lax.dot_general(
        left, right, (((0,), (0,)), ((), ())), preferred_element_type=jnp.float32
    )


def contract_cols(left, right):
    return lax.dot_general(
        left, right, (((1,), (1,)), ((), ())), preferred_element_type=jnp.float32
    )


def place_slice(length, piece, start):
    return lax.dynamic_update_slice_in_dim(jnp.zeros((length,), jnp.float32), piece, start, 0)


def per_device(
    tokens,
    cotangent,
    segment_ids,
    ln1_gain,
    ln1_bias,
    w_query,
    query_bias,
    w_key,
    w_value,
    value_bias,
    w_out,
    out_bias,
    ln2_gain,
    ln2_bias,
    w_in,
    in_bias,
    w_back,
    back_bias,
):
    f32 = jnp.float32
    bf16 = jnp.bfloat16
    index = lax.axis_index("tensor")
    (
        gain_one,
        shift_one,
        full_query,
        qbias_all,
        full_key,
        full_value,
        vbias_all,
        full_out,
        obias_all,
        gain_two,
        shift_two,
        full_in,
        ibias_all,
        full_back,
        bbias_all,
    ) = (
        lax.all_gather(ln1_gain, "dp", axis=0, tiled=True),
        lax.all_gather(ln1_bias, "dp", axis=0, tiled=True),
        lax.all_gather(w_query, "dp", axis=0, tiled=True),
        lax.all_gather(query_bias, "dp", axis=0, tiled=True),
        lax.all_gather(w_key, "dp", axis=0, tiled=True),
        lax.all_gather(w_value, "dp", axis=0, tiled=True),
        lax.all_gather(value_bias, "dp", axis=0, tiled=True),
        lax.all_gather(w_out, "dp", axis=1, tiled=True),
        lax.all_gather(out_bias, "dp", axis=0, tiled=True),
        lax.all_gather(ln2_gain, "dp", axis=0, tiled=True),
        lax.all_gather(ln2_bias, "dp", axis=0, tiled=True),
        lax.all_gather(w_in, "dp", axis=0, tiled=True),
        lax.all_gather(in_bias, "dp", axis=0, tiled=True),
        lax.all_gather(w_back, "dp", axis=1, tiled=True),
        lax.all_gather(back_bias, "dp", axis=0, tiled=True),
    )
    width = tokens.shape[1]
    head_width = full_query.shape[1]
    hidden_width = full_in.shape[1]
    unit_total = ibias_all.shape[0]
    local_heads = head_width // HEAD_DIM
    scale = HEAD_DIM ** (-0.5)
    gain_one = gain_one.astype(f32)
    shift_one = shift_one.astype(f32)
    gain_two = gain_two.astype(f32)
    shift_two = shift_two.astype(f32)
    query_shift = lax.dynamic_slice_in_dim(qbias_all, index * head_width, head_width).astype(f32)
    value_shift = lax.dynamic_slice_in_dim(vbias_all, index * head_width, head_width).astype(f32)
    unit_shift = lax.dynamic_slice_in_dim(ibias_all, index * hidden_width, hidden_width).astype(f32)
    inputs = tokens.astype(f32)
    act_one = layer_norm(inputs, gain_one, shift_one).astype(bf16)
    group_one = lax.all_gather(act_one, "tensor", axis=0, tiled=True)
    merged = jnp.concatenate([full_query, full_key, full_value], axis=1)
    mixed = jnp.dot(group_one, merged, preferred_element_type=f32)
    group = mixed.shape[0]
    seq_count = segment_ids.shape[0]
    seq_len = segment_ids.shape[1]
    query = (mixed[:, :head_width] + query_shift).astype(bf16).reshape(group, local_heads, HEAD_DIM)
    keys = (
        mixed[:, head_width : 2 * head_width]
        .astype(bf16)
        .reshape(seq_count, seq_len, local_heads, HEAD_DIM)
    )
    values = (
        (mixed[:, 2 * head_width :] + value_shift)
        .astype(bf16)
        .reshape(seq_count, seq_len, local_heads, HEAD_DIM)
    )
    block = math.gcd(512, seq_len)
    per_seq = seq_len // block
    block_count = group // block

    def block_scores(number):
        sequence = number // per_seq
        begin = number * block
        offset = begin - sequence * seq_len
        query_block = lax.dynamic_slice_in_dim(query, begin, block, 0)
        key_seq = lax.dynamic_index_in_dim(keys, sequence, 0, keepdims=False)
        value_seq = lax.dynamic_index_in_dim(values, sequence, 0, keepdims=False)
        doc_all = lax.dynamic_index_in_dim(segment_ids, sequence, 0, keepdims=False)
        doc_rows = lax.dynamic_slice_in_dim(doc_all, offset, block, 0)
        raw = jnp.einsum("qhd,khd->hqk", query_block, key_seq, preferred_element_type=f32)
        same = (doc_rows[:, None] == doc_all[None, :])[None]
        scores = jnp.where(same, raw * scale, -1000000000.0)
        return (scores, query_block, key_seq, value_seq, begin, sequence)

    def forward_block(number):
        scores, query_block, key_seq, value_seq, begin, sequence = block_scores(number)
        top = jnp.max(scores, axis=-1, keepdims=True)
        expo = jnp.exp(scores - top)
        denom = jnp.sum(expo, axis=-1, keepdims=True)
        weights = (expo / denom).astype(bf16)
        result = jnp.einsum("hqk,khd->qhd", weights, value_seq, preferred_element_type=f32)
        return (
            result.reshape(block, head_width).astype(bf16),
            top[..., 0] + jnp.log(denom[..., 0]),
        )

    context_blocks, lse_all = lax.map(forward_block, jnp.arange(block_count))
    context = context_blocks.reshape(group, head_width)
    attn_part = jnp.dot(context, full_out, preferred_element_type=f32).astype(bf16)
    attn_sum = lax.psum_scatter(attn_part, "tensor", scatter_dimension=0, tiled=True).astype(
        jnp.float32
    )
    middle = inputs + attn_sum + obias_all.astype(f32)
    act_two = layer_norm(middle, gain_two, shift_two).astype(bf16)
    group_two = lax.all_gather(act_two, "tensor", axis=0, tiled=True)
    pre = jnp.dot(group_two, full_in, preferred_element_type=f32) + unit_shift
    hidden = gelu_exact(pre).astype(bf16)
    mlp_part = jnp.dot(hidden, full_back, preferred_element_type=f32).astype(bf16)
    mlp_sum = lax.psum_scatter(mlp_part, "tensor", scatter_dimension=0, tiled=True).astype(
        jnp.float32
    )
    result = middle + mlp_sum + bbias_all.astype(f32)
    output = result.astype(bf16)
    back_query, back_key, back_value, back_out, back_in, back_back = (
        lax.all_gather(w_query, "dp", axis=0, tiled=True),
        lax.all_gather(w_key, "dp", axis=0, tiled=True),
        lax.all_gather(w_value, "dp", axis=0, tiled=True),
        lax.all_gather(w_out, "dp", axis=1, tiled=True),
        lax.all_gather(w_in, "dp", axis=0, tiled=True),
        lax.all_gather(w_back, "dp", axis=1, tiled=True),
    )
    merged_back = jnp.concatenate([back_query, back_key, back_value], axis=1)
    upstream = cotangent.astype(f32)
    back_bias_term = jnp.sum(upstream, axis=0)
    cot_rows = lax.all_gather(cotangent, "tensor", axis=0, tiled=True)
    grad_w_back = contract_rows(hidden, cot_rows)
    grad_hidden = contract_cols(cot_rows, back_back)
    gelu_out, gelu_pull = jax.vjp(gelu_exact, pre)
    grad_pre = gelu_pull(grad_hidden)[0]
    unit_term = jnp.sum(grad_pre, axis=0)
    pre_low = grad_pre.astype(bf16)
    grad_w_in = contract_rows(group_two, pre_low)
    grad_norm_two = lax.psum_scatter(
        contract_cols(pre_low, back_in).astype(jnp.bfloat16),
        "tensor",
        scatter_dimension=0,
        tiled=True,
    ).astype(jnp.float32)
    norm_out, norm_pull = jax.vjp(layer_norm, middle, gain_two, shift_two)
    grad_mid_norm, ln2_gain_term, ln2_bias_term = norm_pull(grad_norm_two)
    grad_middle = upstream + grad_mid_norm
    out_bias_term = jnp.sum(grad_middle, axis=0)
    middle_low = grad_middle.astype(bf16)
    middle_rows = lax.all_gather(middle_low, "tensor", axis=0, tiled=True)
    grad_w_out = contract_rows(context, middle_rows)
    grad_context = (
        contract_cols(middle_rows, back_out).astype(bf16).reshape(group, local_heads, HEAD_DIM)
    )

    def backward_block(carry, number):
        keys_acc, values_acc = carry
        scores, query_block, key_seq, value_seq, begin, sequence = block_scores(number)
        lse = lax.dynamic_index_in_dim(lse_all, number, 0, keepdims=False)
        probs = jnp.exp(scores - lse[:, :, None])
        weights = probs.astype(bf16)
        upstream_block = lax.dynamic_slice_in_dim(grad_context, begin, block, 0)
        grad_weights = jnp.einsum(
            "qhd,khd->hqk", upstream_block, value_seq, preferred_element_type=f32
        )
        delta = jnp.sum(grad_weights * probs, axis=-1, keepdims=True)
        grad_raw = (probs * (grad_weights - delta) * scale).astype(bf16)
        query_part = jnp.einsum("hqk,khd->qhd", grad_raw, key_seq, preferred_element_type=f32)
        key_part = jnp.einsum("hqk,qhd->khd", grad_raw, query_block, preferred_element_type=f32)
        value_part = jnp.einsum("hqk,qhd->khd", weights, upstream_block, preferred_element_type=f32)
        keys_acc = lax.dynamic_update_index_in_dim(
            keys_acc,
            lax.dynamic_index_in_dim(keys_acc, sequence, 0, keepdims=False) + key_part,
            sequence,
            0,
        )
        values_acc = lax.dynamic_update_index_in_dim(
            values_acc,
            lax.dynamic_index_in_dim(values_acc, sequence, 0, keepdims=False) + value_part,
            sequence,
            0,
        )
        return ((keys_acc, values_acc), query_part)

    empty = jnp.zeros((seq_count, seq_len, local_heads, HEAD_DIM), f32)
    (grad_keys, grad_values), query_parts = lax.scan(
        backward_block, (empty, empty), jnp.arange(block_count)
    )
    grad_query = query_parts.reshape(group, head_width)
    grad_keys = grad_keys.reshape(group, head_width)
    grad_values = grad_values.reshape(group, head_width)
    query_term = jnp.sum(grad_query, axis=0)
    value_term = jnp.sum(grad_values, axis=0)
    grad_lows = jnp.concatenate([grad_query, grad_keys, grad_values], axis=1).astype(bf16)
    grad_merged = contract_rows(group_one, grad_lows)
    grad_w_query = grad_merged[:, :head_width]
    grad_w_key = grad_merged[:, head_width : 2 * head_width]
    grad_w_value = grad_merged[:, 2 * head_width :]
    grad_norm_one = lax.psum_scatter(
        contract_cols(grad_lows, merged_back).astype(jnp.bfloat16),
        "tensor",
        scatter_dimension=0,
        tiled=True,
    ).astype(jnp.float32)
    first_out, first_pull = jax.vjp(layer_norm, inputs, gain_one, shift_one)
    grad_in_norm, ln1_gain_term, ln1_bias_term = first_pull(grad_norm_one)
    grad_tokens = grad_middle + grad_in_norm
    vectors = (
        lax.psum(ln1_gain_term.astype(jnp.bfloat16), "tensor").astype(jnp.float32),
        lax.psum(ln1_bias_term.astype(jnp.bfloat16), "tensor").astype(jnp.float32),
        lax.psum(
            place_slice(width, query_term, index * head_width).astype(jnp.bfloat16), "tensor"
        ).astype(jnp.float32),
        lax.psum(
            place_slice(width, value_term, index * head_width).astype(jnp.bfloat16), "tensor"
        ).astype(jnp.float32),
        lax.psum(out_bias_term.astype(jnp.bfloat16), "tensor").astype(jnp.float32),
        lax.psum(ln2_gain_term.astype(jnp.bfloat16), "tensor").astype(jnp.float32),
        lax.psum(ln2_bias_term.astype(jnp.bfloat16), "tensor").astype(jnp.float32),
        lax.psum(
            place_slice(unit_total, unit_term, index * hidden_width).astype(jnp.bfloat16), "tensor"
        ).astype(jnp.float32),
        lax.psum(back_bias_term.astype(jnp.bfloat16), "tensor").astype(jnp.float32),
    )
    (
        grad_w_query,
        grad_w_key,
        grad_w_value,
        grad_w_out,
        grad_w_in,
        grad_w_back,
        grad_ln1_gain,
        grad_ln1_bias,
        grad_query_bias,
        grad_value_bias,
        grad_out_bias,
        grad_ln2_gain,
        grad_ln2_bias,
        grad_in_bias,
        grad_back_bias,
    ) = (
        lax.psum_scatter(grad_w_query, "dp", scatter_dimension=0, tiled=True),
        lax.psum_scatter(grad_w_key, "dp", scatter_dimension=0, tiled=True),
        lax.psum_scatter(grad_w_value, "dp", scatter_dimension=0, tiled=True),
        lax.psum_scatter(grad_w_out, "dp", scatter_dimension=1, tiled=True),
        lax.psum_scatter(grad_w_in, "dp", scatter_dimension=0, tiled=True),
        lax.psum_scatter(grad_w_back, "dp", scatter_dimension=1, tiled=True),
        lax.psum_scatter(vectors[0], "dp", scatter_dimension=0, tiled=True),
        lax.psum_scatter(vectors[1], "dp", scatter_dimension=0, tiled=True),
        lax.psum_scatter(vectors[2], "dp", scatter_dimension=0, tiled=True),
        lax.psum_scatter(vectors[3], "dp", scatter_dimension=0, tiled=True),
        lax.psum_scatter(vectors[4], "dp", scatter_dimension=0, tiled=True),
        lax.psum_scatter(vectors[5], "dp", scatter_dimension=0, tiled=True),
        lax.psum_scatter(vectors[6], "dp", scatter_dimension=0, tiled=True),
        lax.psum_scatter(vectors[7], "dp", scatter_dimension=0, tiled=True),
        lax.psum_scatter(vectors[8], "dp", scatter_dimension=0, tiled=True),
    )
    return (
        output,
        grad_tokens,
        grad_ln1_gain,
        grad_ln1_bias,
        grad_w_query,
        grad_query_bias,
        grad_w_key,
        grad_w_value,
        grad_value_bias,
        grad_w_out,
        grad_out_bias,
        grad_ln2_gain,
        grad_ln2_bias,
        grad_w_in,
        grad_in_bias,
        grad_w_back,
        grad_back_bias,
    )


def solution(mesh):
    return jax.shard_map(
        per_device,
        mesh=mesh,
        in_specs=(
            P(("dp", "tensor"), None),
            P(("dp", "tensor"), None),
            P("dp", None),
            P("dp"),
            P("dp"),
            P("dp", "tensor"),
            P("dp"),
            P("dp", "tensor"),
            P("dp", "tensor"),
            P("dp"),
            P("tensor", "dp"),
            P("dp"),
            P("dp"),
            P("dp"),
            P("dp", "tensor"),
            P("dp"),
            P("tensor", "dp"),
            P("dp"),
        ),
        out_specs=(
            P(("dp", "tensor"), None),
            P(("dp", "tensor"), None),
            P("dp"),
            P("dp"),
            P("dp", "tensor"),
            P("dp"),
            P("dp", "tensor"),
            P("dp", "tensor"),
            P("dp"),
            P("tensor", "dp"),
            P("dp"),
            P("dp"),
            P("dp"),
            P("dp", "tensor"),
            P("dp"),
            P("tensor", "dp"),
            P("dp"),
        ),
        check_vma=False,
    )
```

profile of v0, /device:TPU:0, one launch (start us, length us, event | category | flops | bytes accessed | tf_op | source)
XLA Modules:
  0.0 1247.8 jit_solution(12022204815762069830)
XLA Ops:
  19.7 39.5 %all-reduce.18 = (bf16[768]{0:T(1024)(128)(2,1)S(1)}, bf16[768]{0:T(1024)(128)(2,1)S(1)}, bf16[768]{0:T(1024)(128)(2,1)S(1)}, bf16[768]{0:T(1024)(128)(2,1)S(1)}...) all-reduce(bf16[768]{0:T(1024)(128)(2,1)S(1)} %dynamic-update-slice, ...), channel_id=1, replica_groups=mesh['dp'=8,'tensor'=4] {'dp'}, use_global_device_ids=true, to_apply=%add.1 | all-reduce | flops 6144 | bytes 24576
  62.5 31.0 %all_gather.71 = bf16[192,768]{0,1:T(8,128)(2,1)S(1)} all-gather(bf16[192,96]{0,1:T(8,128)(2,1)S(1)} %copy.44), channel_id=1, replica_groups=mesh['dp'=8,'tensor'=4] {'dp'}, dimensions={1}, use_global_device_ids=true | all-gather | bytes 331776 | tf_op jit(solution)/shard_map/all_gather | solution.py:84
  93.5 31.0 %all_gather.66 = bf16[768,192]{1,0:T(8,128)(2,1)S(1)} all-gather(bf16[96,192]{1,0:T(8,128)(2,1)S(1)} %copy-done.36), channel_id=1, replica_groups=mesh['dp'=8,'tensor'=4] {'dp'}, dimensions={0}, use_global_device_ids=true | all-gather | bytes 331776 | tf_op jit(solution)/shard_map/all_gather | solution.py:79
  124.5 31.0 %all_gather.67 = bf16[768,192]{1,0:T(8,128)(2,1)S(1)} all-gather(bf16[96,192]{1,0:T(8,128)(2,1)S(1)} %copy-done.37), channel_id=1, replica_groups=mesh['dp'=8,'tensor'=4] {'dp'}, dimensions={0}, use_global_device_ids=true | all-gather | bytes 331776 | tf_op jit(solution)/shard_map/all_gather | solution.py:81
  155.5 31.1 %all_gather.68 = bf16[768,192]{1,0:T(8,128)(2,1)S(1)} all-gather(bf16[96,192]{1,0:T(8,128)(2,1)S(1)} %copy-done.38), channel_id=1, replica_groups=mesh['dp'=8,'tensor'=4] {'dp'}, dimensions={0}, use_global_device_ids=true | all-gather | bytes 331776 | tf_op jit(solution)/shard_map/all_gather | solution.py:82
  191.6 98.7 %while.30 = (s32[]{:T(128)}, bf16[4,512,192]{1,2,0:T(8,128)(2,1)}, f32[4,3,512]{2,1,0:T(4,128)S(1)}, s32[4]{0:T(128)S(1)}, s32[1,2048]{1,0:T(1,128)S(1)}, /*inde...) while((s32[]{:T(128)}, bf16[4,512,192]{1,2,0:T(8,128)(2,1)}, ...), condition=%wide.region_5.6_spmd, body=%wide.region_2.5_spmd.sunk | while | flops 844200448 | bytes 44372400 | solution.py:155
  296.1 34.7 %reduce-scatter.19.cloned.1.call-done = bf16[512,768]{1,0:T(8,128)(2,1)} async-done(((bf16[2048,768]{1,0:T(8,128)(2,1)}), bf16[512,768]{1,0:T(8,128)(2,1)}) %reduce-scatter.19.cloned.1.call-update) | async-done | bytes 786448 | tf_op jit(solution)/shard_map/reduce_scatter | solution.py:158
  336.7 26.4 %all-gather = bf16[8,1,384]{2,1,0:T(2,128)(2,1)S(1)} all-gather(bf16[1,1,384]{2,1,0:T(2,128)(2,1)S(1)} %reshape.282), channel_id=1, replica_groups=mesh['dp'=8,'tensor'=4] {'dp'}, dimensions={0}, use_global_device_ids=true | all-gather | bytes 6912 | tf_op jit(solution)/shard_map/all_gather | solution.py:89
  366.1 7.6 fusion.135
  373.6 36.3 %all-gather.14.cloned.1.call-done = bf16[768,768]{0,1:T(8,128)(2,1)} async-done(((bf16[768,96]{0,1:T(8,128)(2,1)}), bf16[768,768]{0,1:T(8,128)(2,1)}) %all-gather.14.cloned.1.call-update) | async-done | bytes 1179664 | tf_op jit(solution)/shard_map/all_gather | solution.py:90
  409.9 28.5 %all-gather.16.cloned.1.call-done = bf16[2048,768]{1,0:T(8,128)(2,1)} async-done(((bf16[512,768]{1,0:T(8,128)(2,1)}), bf16[2048,768]{1,0:T(8,128)(2,1)}) %all-gather.16.cloned.1.call-update) | async-done | bytes 3145744 | tf_op jit(solution)/shard_map/all_gather | solution.py:183
  438.5 20.5 %fusion.128 = (bf16[768]{0:T(1024)(128)(2,1)}, bf16[2048,768]{1,0:T(8,128)(2,1)S(1)}, f32[2048,768]{1,0:T(8,128)}) fusion(f32[2048,768]{1,0:T(8,128)} %fusion.135, f32[768]{0:T(1024)S(1)} %dynamic-slice_convert_fusion, bf16[2048,768]{1,0:T(8,128)(2,1)} %all-gather.16.cloned.1.call-done, bf16[768,768]{0,1:T(8,128)(2,1)} %all-gather.14.cloned.1.call-done), kind=kOutput, calls=%fused_computation.153 | convolution fusion | flops 2532310272 | bytes 20058624 | tf_op jit(solution)/shard_map/dot_general | solution.py:28
  476.8 26.1 %reduce-scatter.23.cloned.1.call-done = bf16[512,768]{1,0:T(8,128)(2,1)} async-done(((bf16[2048,768]{1,0:T(8,128)(2,1)}), bf16[512,768]{1,0:T(8,128)(2,1)}) %reduce-scatter.23.cloned.1.call-update) | async-done | bytes 786448 | tf_op jit(solution)/shard_map/reduce_scatter | solution.py:191
  507.4 35.9 %reduce-scatter.21.cloned.1.call-done = bf16[512,768]{1,0:T(8,128)(2,1)} async-done(((bf16[2048,768]{1,0:T(8,128)(2,1)}), bf16[512,768]{1,0:T(8,128)(2,1)}) %reduce-scatter.21.cloned.1.call-update) | async-done | bytes 786448 | tf_op jit(solution)/shard_map/reduce_scatter | solution.py:167
  549.5 28.4 %all-gather.18.cloned.1.call-done = bf16[2048,768]{1,0:T(8,128)(2,1)} async-done(((bf16[512,768]{1,0:T(8,128)(2,1)}), bf16[2048,768]{1,0:T(8,128)(2,1)}) %all-gather.18.cloned.1.call-update) | async-done | bytes 3145744 | tf_op jit(solution)/shard_map/all_gather | solution.py:202
  588.9 258.0 %while.31 = (s32[]{:T(128)}, f32[1,2048,3,64]{1,3,2,0:T(8,128)}, f32[1,2048,3,64]{1,3,2,0:T(8,128)}, f32[4,512,3,64]{1,3,2,0:T(8,128)}, s32[4]{0:T(128)S(1)}, /*...) while((s32[]{:T(128)}, f32[1,2048,3,64]{1,3,2,0:T(8,128)}, ...), condition=%wide.region_15.16_spmd, body=%wide.region_13.15_spmd.sunk | while | flops 2096897024 | bytes 208079408 | solution.py:238
  610.3 20.9 %fusion.194 = f32[4,512,3,64]{1,3,2,0:T(8,128)} fusion(f32[4,512,3,64]{1,3,2,0:T(8,128)} %get-tuple-element.595, s32[]{:T(128)S(6)} %copy.83, f32[3,512,2048]{2,1,0:T(8,128)} %fusion.190, f32[3,512,2048]{2,1,0:T(8,128)} %copy-done, f32[3,512]{1,0:T(4,128)S(1)} %dynamic-slice_bitcast_fusion.2, pred[512,2048]{1,0:T(8,128)(4,1)S(1)} %broadcast_compare_fusion.5, ...), kind=kOutput, calls=%fused_computation.44.clone.1 | convolution fusion | flops 437259776 | bytes 53624836 | tf_op jit(solution)/shard_map/while/body/eval_jaxpr/hqk,khd->qhd/dot_general | solution.py:220
  631.2 22.6 %fusion.192 = f32[1,2048,3,64]{1,3,2,0:T(8,128)} fusion(f32[3,512,2048]{2,1,0:T(8,128)} %fusion.190, f32[3,512,2048]{2,1,0:T(8,128)} %copy-done, f32[3,512]{1,0:T(4,128)S(1)} %dynamic-slice_bitcast_fusion.2, pred[512,2048]{1,0:T(8,128)(4,1)S(1)} %broadcast_compare_fusion.5, f32[1,2048,3,64]{1,3,2,0:T(8,128)} %get-tuple-element.593, ...), kind=kOutput, calls=%fused_computation.39.clone.1 | convolution fusion | flops 437652992 | bytes 55787524 | tf_op jit(solution)/shard_map/while/body/eval_jaxpr/hqk,qhd->khd/dot_general | solution.py:221
  675.0 20.7 %fusion.194 = f32[4,512,3,64]{1,3,2,0:T(8,128)} fusion(f32[4,512,3,64]{1,3,2,0:T(8,128)} %get-tuple-element.595, s32[]{:T(128)S(6)} %copy.83, f32[3,512,2048]{2,1,0:T(8,128)} %fusion.190, f32[3,512,2048]{2,1,0:T(8,128)} %copy-done, f32[3,512]{1,0:T(4,128)S(1)} %dynamic-slice_bitcast_fusion.2, pred[512,2048]{1,0:T(8,128)(4,1)S(1)} %broadcast_compare_fusion.5, ...), kind=kOutput, calls=%fused_computation.44.clone.1 | convolution fusion | flops 437259776 | bytes 53624836 | tf_op jit(solution)/shard_map/while/body/eval_jaxpr/hqk,khd->qhd/dot_general | solution.py:220
  695.7 22.4 %fusion.192 = f32[1,2048,3,64]{1,3,2,0:T(8,128)} fusion(f32[3,512,2048]{2,1,0:T(8,128)} %fusion.190, f32[3,512,2048]{2,1,0:T(8,128)} %copy-done, f32[3,512]{1,0:T(4,128)S(1)} %dynamic-slice_bitcast_fusion.2, pred[512,2048]{1,0:T(8,128)(4,1)S(1)} %broadcast_compare_fusion.5, f32[1,2048,3,64]{1,3,2,0:T(8,128)} %get-tuple-element.593, ...), kind=kOutput, calls=%fused_computation.39.clone.1 | convolution fusion | flops 437652992 | bytes 55787524 | tf_op jit(solution)/shard_map/while/body/eval_jaxpr/hqk,qhd->khd/dot_general | solution.py:221
  739.2 20.7 %fusion.194 = f32[4,512,3,64]{1,3,2,0:T(8,128)} fusion(f32[4,512,3,64]{1,3,2,0:T(8,128)} %get-tuple-element.595, s32[]{:T(128)S(6)} %copy.83, f32[3,512,2048]{2,1,0:T(8,128)} %fusion.190, f32[3,512,2048]{2,1,0:T(8,128)} %copy-done, f32[3,512]{1,0:T(4,128)S(1)} %dynamic-slice_bitcast_fusion.2, pred[512,2048]{1,0:T(8,128)(4,1)S(1)} %broadcast_compare_fusion.5, ...), kind=kOutput, calls=%fused_computation.44.clone.1 | convolution fusion | flops 437259776 | bytes 53624836 | tf_op jit(solution)/shard_map/while/body/eval_jaxpr/hqk,khd->qhd/dot_general | solution.py:220
  760.0 22.4 %fusion.192 = f32[1,2048,3,64]{1,3,2,0:T(8,128)} fusion(f32[3,512,2048]{2,1,0:T(8,128)} %fusion.190, f32[3,512,2048]{2,1,0:T(8,128)} %copy-done, f32[3,512]{1,0:T(4,128)S(1)} %dynamic-slice_bitcast_fusion.2, pred[512,2048]{1,0:T(8,128)(4,1)S(1)} %broadcast_compare_fusion.5, f32[1,2048,3,64]{1,3,2,0:T(8,128)} %get-tuple-element.593, ...), kind=kOutput, calls=%fused_computation.39.clone.1 | convolution fusion | flops 437652992 | bytes 55787524 | tf_op jit(solution)/shard_map/while/body/eval_jaxpr/hqk,qhd->khd/dot_general | solution.py:221
  803.6 20.8 %fusion.194 = f32[4,512,3,64]{1,3,2,0:T(8,128)} fusion(f32[4,512,3,64]{1,3,2,0:T(8,128)} %get-tuple-element.595, s32[]{:T(128)S(6)} %copy.83, f32[3,512,2048]{2,1,0:T(8,128)} %fusion.190, f32[3,512,2048]{2,1,0:T(8,128)} %copy-done, f32[3,512]{1,0:T(4,128)S(1)} %dynamic-slice_bitcast_fusion.2, pred[512,2048]{1,0:T(8,128)(4,1)S(1)} %broadcast_compare_fusion.5, ...), kind=kOutput, calls=%fused_computation.44.clone.1 | convolution fusion | flops 437259776 | bytes 53624836 | tf_op jit(solution)/shard_map/while/body/eval_jaxpr/hqk,khd->qhd/dot_general | solution.py:220
  824.3 22.4 %fusion.192 = f32[1,2048,3,64]{1,3,2,0:T(8,128)} fusion(f32[3,512,2048]{2,1,0:T(8,128)} %fusion.190, f32[3,512,2048]{2,1,0:T(8,128)} %copy-done, f32[3,512]{1,0:T(4,128)S(1)} %dynamic-slice_bitcast_fusion.2, pred[512,2048]{1,0:T(8,128)(4,1)S(1)} %broadcast_compare_fusion.5, f32[1,2048,3,64]{1,3,2,0:T(8,128)} %get-tuple-element.593, ...), kind=kOutput, calls=%fused_computation.39.clone.1 | convolution fusion | flops 437652992 | bytes 55787524 | tf_op jit(solution)/shard_map/while/body/eval_jaxpr/hqk,qhd->khd/dot_general | solution.py:221
  887.3 9.5 reduce-scatter.25.cloned.1.call-done
  901.8 10.3 all-reduce.19
  912.1 38.8 %all-reduce.17 = (f32[768]{0:T(1024)S(1)}, f32[768]{0:T(1024)S(1)}, f32[768]{0:T(1024)S(1)}, f32[768]{0:T(1024)S(1)}, f32[768]{0:T(1024)S(1)}, /*index=5*/f32[76...) all-reduce(bf16[768]{0:T(1024)(128)(2,1)S(1)} %get-tuple-element.37, ...), channel_id=6, replica_groups=mesh['dp'=8,'tensor'=4] {'dp'}, use_global_device_ids=true, to_apply=%region_21.22.clone | all-reduce | flops 9216 | bytes 55296
  958.0 12.7 %reduce-scatter.29.cloned.1.call-done = f32[768,96]{0,1:T(8,128)} async-done(((f32[768,768]{0,1:T(8,128)}), f32[768,96]{0,1:T(8,128)}) %reduce-scatter.29.cloned.1.call-update) | async-done | bytes 294928 | tf_op jit(solution)/shard_map/reduce_scatter | solution.py:299
  970.7 72.6 %reduce-scatter.27.cloned.1.call-done = f32[96,768]{1,0:T(8,128)} async-done(((f32[768,768]{1,0:T(8,128)}), f32[96,768]{1,0:T(8,128)}) %reduce-scatter.27.cloned.1.call-update) | async-done | bytes 294928 | tf_op jit(solution)/shard_map/reduce_scatter | solution.py:298
  1043.2 65.9 %reduce-scatter.35.cloned.1.call-done = f32[96,192]{1,0:T(8,128)} async-done(((f32[768,192]{1,0:T(8,128)}), f32[96,192]{1,0:T(8,128)}) %reduce-scatter.35.cloned.1.call-update) | async-done | bytes 73744
  1109.2 65.4 %reduce-scatter.33.cloned.1.call-done = f32[96,192]{1,0:T(8,128)} async-done(((f32[768,192]{1,0:T(8,128)}), f32[96,192]{1,0:T(8,128)}) %reduce-scatter.33.cloned.1.call-update) | async-done | bytes 73744
  1174.5 65.9 %reduce-scatter.31.cloned.1.call-done = f32[96,192]{1,0:T(8,128)} async-done(((f32[768,192]{1,0:T(8,128)}), f32[96,192]{1,0:T(8,128)}) %reduce-scatter.31.cloned.1.call-update) | async-done | bytes 73744
  (313 shorter events, 275.7 us)
Async XLA Ops:
  8.0 54.3 %copy-start.39 = (bf16[192,96]{1,0:T(8,128)(2,1)S(1)}, bf16[192,96]{1,0:T(8,128)(2,1)}, u32[]{:S(2)}) copy-start(bf16[192,96]{1,0:T(8,128)(2,1)} %param.32) | copy-start | bytes 110596
  8.0 85.5 %copy-start.36 = (bf16[96,192]{1,0:T(8,128)(2,1)S(1)}, bf16[96,192]{1,0:T(8,128)(2,1)}, u32[]{:S(2)}) copy-start(bf16[96,192]{1,0:T(8,128)(2,1)} %param.27) | copy-start | bytes 110596
  8.0 116.4 %copy-start.37 = (bf16[96,192]{1,0:T(8,128)(2,1)S(1)}, bf16[96,192]{1,0:T(8,128)(2,1)}, u32[]{:S(2)}) copy-start(bf16[96,192]{1,0:T(8,128)(2,1)} %param.29) | copy-start | bytes 110596
  8.1 147.4 %copy-start.38 = (bf16[96,192]{1,0:T(8,128)(2,1)S(1)}, bf16[96,192]{1,0:T(8,128)(2,1)}, u32[]{:S(2)}) copy-start(bf16[96,192]{1,0:T(8,128)(2,1)} %param.30) | copy-start | bytes 110596
  8.1 178.5 %all-gather.8.cloned.1.call-start = ((), (), s32[]{:S(2)}) async-start(), calls=%async_computation.10 | async-start | bytes 3932160 | tf_op jit(solution)/shard_map/all_gather | solution.py:108
  9.4 52.8 %copy-start.34 = (f32[512]{0:T(512)}, f32[512]{0:T(512)S(1)}, u32[]{:S(2)}) copy-start(f32[512]{0:T(512)S(1)} %broadcast_multiply_fusion.1) | copy-start | bytes 6148
  10.9 51.3 %copy-start.42 = (f32[512]{0:T(512)}, f32[512]{0:T(512)S(1)}, u32[]{:S(2)}) copy-start(f32[512]{0:T(512)S(1)} %fusion.109) | copy-start | bytes 6148
  11.0 51.3 %copy-start.40 = (f32[512]{0:T(512)}, f32[512]{0:T(512)S(1)}, u32[]{:S(2)}) copy-start(f32[512]{0:T(512)S(1)} %fusion.122) | copy-start | bytes 6148
  62.2 268.6 %reduce-scatter.19.cloned.1.call-start = ((), (), s32[]{:S(2)}) async-start(), calls=%async_computation.11 | async-start | bytes 3932160 | tf_op jit(solution)/shard_map/reduce_scatter | solution.py:158
  93.5 198.3 %copy-start.13 = (bf16[192,768]{0,1:T(8,128)(2,1)}, bf16[192,768]{0,1:T(8,128)(2,1)S(1)}, u32[]{:S(2)}) copy-start(bf16[192,768]{0,1:T(8,128)(2,1)S(1)} %all_gather.71) | copy-start | bytes 884740
  124.5 62.1 %copy-start.26 = (bf16[768,192]{1,0:T(8,128)(2,1)}, bf16[768,192]{1,0:T(8,128)(2,1)S(1)}, u32[]{:S(2)}) copy-start(bf16[768,192]{1,0:T(8,128)(2,1)S(1)} %all_gather.66) | copy-start | bytes 884740
  155.5 31.1 %copy-start.28 = (bf16[768,192]{1,0:T(8,128)(2,1)}, bf16[768,192]{1,0:T(8,128)(2,1)S(1)}, u32[]{:S(2)}) copy-start(bf16[768,192]{1,0:T(8,128)(2,1)S(1)} %all_gather.67) | copy-start | bytes 884740
  292.7 38.1 %copy-start.1 = (bf16[512,768]{1,0:T(8,128)(2,1)S(1)}, bf16[512,768]{1,0:T(8,128)(2,1)}, u32[]{:S(2)}) copy-start(bf16[512,768]{1,0:T(8,128)(2,1)} %param.22) | copy-start | bytes 2359300
  295.4 67.8 %all-gather.12.cloned.1.call-start = ((), (), s32[]{:S(2)}) async-start(), calls=%async_computation.13 | async-start | bytes 1327104 | tf_op jit(solution)/shard_map/all_gather | solution.py:88
  296.0 70.1 %all-gather.10.cloned.1.call-start = ((), (), s32[]{:S(2)}) async-start(), calls=%async_computation.12 | async-start | bytes 3932160 | tf_op jit(solution)/shard_map/all_gather | solution.py:163
  335.3 74.6 %all-gather.14.cloned.1.call-start = ((), (), s32[]{:S(2)}) async-start(), calls=%async_computation.14 | async-start | bytes 1327104 | tf_op jit(solution)/shard_map/all_gather | solution.py:90
  335.9 102.6 %all-gather.16.cloned.1.call-start = ((), (), s32[]{:S(2)}) async-start(), calls=%async_computation.16 | async-start | bytes 3932160 | tf_op jit(solution)/shard_map/all_gather | solution.py:183
  336.7 166.2 %reduce-scatter.23.cloned.1.call-start = ((), (), s32[]{:S(2)}) async-start(), calls=%async_computation.17 | async-start | bytes 3932160 | tf_op jit(solution)/shard_map/reduce_scatter | solution.py:191
  438.5 22.3 %copy-start.49 = (bf16[768,768]{1,0:T(8,128)(2,1)S(1)}, bf16[768,768]{1,0:T(8,128)(2,1)}, u32[]{:S(2)}) copy-start(bf16[768,768]{1,0:T(8,128)(2,1)} %all-gather.12.cloned.1.call-done) | copy-start | bytes 3538948
  464.8 78.5 %reduce-scatter.21.cloned.1.call-start = ((), (), s32[]{:S(2)}) async-start(), calls=%async_computation.15 | async-start | bytes 3932160 | tf_op jit(solution)/shard_map/reduce_scatter | solution.py:167
  476.1 101.8 %all-gather.18.cloned.1.call-start = ((), (), s32[]{:S(2)}) async-start(), calls=%async_computation.18 | async-start | bytes 3932160 | tf_op jit(solution)/shard_map/all_gather | solution.py:202
  547.3 30.7 %copy-start.18 = (bf16[4,24,8,512]{3,2,0,1:T(8,128)(2,1)S(1)}, bf16[4,24,8,512]{3,2,0,1:T(8,128)(2,1)}, u32[]{:S(2)}) copy-start(bf16[4,24,8,512]{3,2,0,1:T(8,128)(2,1)} %copy-done.17) | copy-start | bytes 2359300
  549.4 336.2 %reduce-scatter.37.cloned.1.call-start = ((), (), s32[]{:S(2)}) async-start(), calls=%async_computation.25 | async-start | bytes 884736
  549.5 32.6 %copy-start.14 = (bf16[192,768]{0,1:T(8,128)(2,1)S(1)}, bf16[192,768]{0,1:T(8,128)(2,1)}, u32[]{:S(2)}) copy-start(bf16[192,768]{0,1:T(8,128)(2,1)} %copy-done.13) | copy-start | bytes 884740
  582.1 314.7 %reduce-scatter.25.cloned.1.call-start = ((), (), s32[]{:S(2)}) async-start(), calls=%async_computation.19 | async-start | bytes 3932160 | tf_op jit(solution)/shard_map/reduce_scatter | solution.py:251
  858.8 111.9 %reduce-scatter.29.cloned.1.call-start = ((), (), s32[]{:S(2)}) async-start(), calls=%async_computation.21 | async-start | bytes 2654208 | tf_op jit(solution)/shard_map/reduce_scatter | solution.py:299
  866.7 176.5 %reduce-scatter.27.cloned.1.call-start = ((), (), s32[]{:S(2)}) async-start(), calls=%async_computation.20 | async-start | bytes 2654208 | tf_op jit(solution)/shard_map/reduce_scatter | solution.py:298
  874.3 234.8 %reduce-scatter.35.cloned.1.call-start = ((), (), s32[]{:S(2)}) async-start(), calls=%async_computation.24 | async-start | bytes 884736
  879.6 294.9 %reduce-scatter.33.cloned.1.call-start = ((), (), s32[]{:S(2)}) async-start(), calls=%async_computation.23 | async-start | bytes 884736
  880.9 359.5 %reduce-scatter.31.cloned.1.call-start = ((), (), s32[]{:S(2)}) async-start(), calls=%async_computation.22 | async-start | bytes 884736
  884.0 72.3 %copy-start.5 = (f32[512,768]{1,0:T(8,128)S(1)}, f32[512,768]{1,0:T(8,128)}, u32[]{:S(2)}) copy-start(f32[512,768]{1,0:T(8,128)} %copy-done.4) | copy-start | bytes 4718596
  896.7 59.5 %copy-start.7 = (bf16[512,768]{1,0:T(8,128)(2,1)S(1)}, bf16[512,768]{1,0:T(8,128)(2,1)}, u32[]{:S(2)}) copy-start(bf16[512,768]{1,0:T(8,128)(2,1)} %reduce-scatter.25.cloned.1.call-done) | copy-start | bytes 2359300
  (42 other events, 258.1 us)
Sparse Core Ops, SparseCore 0:
  62.3 25.7 all-gather.7
  295.5 35.2 reduce-scatter.18
  464.9 37.9 reduce-scatter.22
  505.2 37.9 reduce-scatter.20
Sparse Core Ops, SparseCore 1:
  298.3 38.8 all-gather.11
  339.2 26.8 all-gather.9
  368.4 41.5 all-gather.13
  411.6 26.8 all-gather.15
  549.5 28.3 all-gather.17
  582.1 62.5 reduce-scatter.36
  858.9 37.8 reduce-scatter.24
  901.1 69.5 reduce-scatter.28
  975.0 68.2 reduce-scatter.26
  1047.5 61.6 reduce-scatter.34
  1112.9 61.6 reduce-scatter.32
  1178.8 61.6 reduce-scatter.30
where the time goes:
time: 1250 us
  waiting for transfers between devices  487 us (39%)
  matrix products  358 us (29%)
  blocking collectives  239 us (19%)
  other arithmetic  70.1 us (6%)
  local copies, waits for them, and re-layouts  42.9 us (3%)
  loops' own time  31.9 us (3%)
  between operations  18.4 us (1%)
    unnamed x20, waiting for transfers between devices  199 us
    dot_general x4, matrix products, backward_block(): jnp.einsum('hqk,qhd->khd', grad_raw, query_block, preferred_element_type=...  89.7 us
    dot_general x4, matrix products, backward_block(): jnp.einsum('hqk,khd->qhd', grad_raw, key_seq, preferred_element_type=f32)  83.1 us
    unnamed x2, blocking collectives  78.3 us
    reduce_scatter x1, waiting for transfers between devices, per_device(): lax.psum_scatter(grad_w_in, 'dp', scatter_dimension=0, tiled=True)  72.6 us
    all_gather x1, waiting for transfers between devices, per_device(): lax.all_gather(w_back, 'dp', axis=1, tiled=True)  36.3 us
    reduce_scatter x1, waiting for transfers between devices, per_device(): lax.psum_scatter(mlp_part, 'tensor', scatter_dimension=0, tiled=True)  35.9 us
    reduce_scatter x1, waiting for transfers between devices, per_device(): lax.psum_scatter(attn_part, 'tensor', scatter_dimension=0, tiled=True)  34.7 us
  transfers between devices with their start and end apart: 16, of which 13 were waited for; matrix products, arithmetic and copies ran while one was open for 26% of the time, Pallas kernels for 0%

commit v1 on v0

--- a/solution.py
+++ b/solution.py
@@ -6,6 +6,23 @@
 
 HEAD_DIM = 64
 EPSILON = 1e-12
+
+
+def in_order(blocks, dim):
+    shape = list(blocks.shape[1:])
+    shape[dim] *= blocks.shape[0]
+    return jnp.moveaxis(blocks, 0, dim).reshape(shape)
+
+
+def ring_gather(x, axis, dim):
+    size = lax.axis_size(axis)
+    upward = [(i, (i + 1) % size) for i in range(size)]
+    tiles = [x]
+    while len(tiles) < size:
+        tiles.append(lax.ppermute(tiles[-1], axis, upward))
+    index = lax.axis_index(axis)
+    tiles = jnp.stack(tiles)[(index - jnp.arange(size)) % size]
+    return in_order(tiles, dim)
 
 
 def layer_norm(values, gain, shift):
@@ -78,7 +95,7 @@
         lax.all_gather(ln1_bias, "dp", axis=0, tiled=True),
         lax.all_gather(w_query, "dp", axis=0, tiled=True),
         lax.all_gather(query_bias, "dp", axis=0, tiled=True),
-        lax.all_gather(w_key, "dp", axis=0, tiled=True),
+        ring_gather(w_key, "dp", 0),
         lax.all_gather(w_value, "dp", axis=0, tiled=True),
         lax.all_gather(value_bias, "dp", axis=0, tiled=True),
         lax.all_gather(w_out, "dp", axis=1, tiled=True),

time: 1250 us -> 1270 us (1.016)
    ppermute x0 -> x7, waiting for transfers between devices: none -> 38.8 us  [ring_gather(): tiles.append(lax.ppermute(tiles[-1], axis, upward))]
    all_gather x1, waiting for transfers between devices: 28.4 us -> 0.01 us  [per_device(): middle_rows = lax.all_gather(middle_low, 'tensor', axis=0, tiled=True)]
    unnamed x134 -> x127, local copies, waits for them, and re-layouts: 28.6 us -> 25.2 us
  transfers between devices with their start and end apart: 16 -> 23, of which waited for: 13 -> 18; matrix products, arithmetic and copies ran while one was open for 26% -> 25% of each run, Pallas kernels for 0% -> 0%
where the time goes in v1:
time: 1270 us; the launch traced here: 1260 us
  waiting for transfers between devices  498 us (39%)
  matrix products  359 us (28%)
  blocking collectives  241 us (19%)
  other arithmetic  69.6 us (5%)
  local copies, waits for them, and re-layouts  40.1 us (3%)
  loops' own time  31.9 us (3%)
  between operations  18.5 us (1%)
    unnamed x20, waiting for transfers between devices  199 us
    dot_general x4, matrix products, backward_block(): jnp.einsum('hqk,qhd->khd', grad_raw, query_block, preferred_element_type=...  89.7 us
    dot_general x4, matrix products, backward_block(): jnp.einsum('hqk,khd->qhd', grad_raw, key_seq, preferred_element_type=f32)  83.1 us
    unnamed x2, blocking collectives  77.6 us
    reduce_scatter x1, waiting for transfers between devices, per_device(): lax.psum_scatter(grad_w_in, 'dp', scatter_dimension=0, tiled=True)  72.3 us
    ppermute x7, waiting for transfers between devices, ring_gather(): tiles.append(lax.ppermute(tiles[-1], axis, upward))  38.8 us
    all_gather x1, waiting for transfers between devices, per_device(): lax.all_gather(w_back, 'dp', axis=1, tiled=True)  36.3 us
    reduce_scatter x1, waiting for transfers between devices, per_device(): lax.psum_scatter(mlp_part, 'tensor', scatter_dimension=0, tiled=True)  35.9 us
  transfers between devices with their start and end apart: 23, of which 18 were waited for; matrix products, arithmetic and copies ran while one was open for 25% of the time, Pallas kernels for 0%

profile of v1, /device:TPU:0, one launch (start us, length us, event | category | flops | bytes accessed | tf_op | source)
XLA Modules:
  0.0 1260.6 jit_solution(5303639133420362494)
XLA Ops:
  19.7 39.4 %all-reduce.18 = (bf16[768]{0:T(1024)(128)(2,1)S(1)}, bf16[768]{0:T(1024)(128)(2,1)S(1)}, bf16[768]{0:T(1024)(128)(2,1)S(1)}, bf16[768]{0:T(1024)(128)(2,1)S(1)}...) all-reduce(bf16[768]{0:T(1024)(128)(2,1)S(1)} %dynamic-update-slice, ...), channel_id=1, replica_groups=mesh['dp'=8,'tensor'=4] {'dp'}, use_global_device_ids=true, to_apply=%add.1 | all-reduce | flops 6144 | bytes 24576
  61.8 31.0 %all_gather.69 = bf16[192,768]{0,1:T(8,128)(2,1)S(1)} all-gather(bf16[192,96]{0,1:T(8,128)(2,1)S(1)} %copy.44), channel_id=1, replica_groups=mesh['dp'=8,'tensor'=4] {'dp'}, dimensions={1}, use_global_device_ids=true | all-gather | bytes 331776 | tf_op jit(solution)/shard_map/all_gather | solution.py:101
  92.8 31.4 %all_gather.65 = bf16[768,192]{1,0:T(8,128)(2,1)S(1)} all-gather(bf16[96,192]{1,0:T(8,128)(2,1)S(1)} %copy-done.30), channel_id=1, replica_groups=mesh['dp'=8,'tensor'=4] {'dp'}, dimensions={0}, use_global_device_ids=true | all-gather | bytes 331776 | tf_op jit(solution)/shard_map/all_gather | solution.py:96
  124.2 31.0 %all_gather.66 = bf16[768,192]{1,0:T(8,128)(2,1)S(1)} all-gather(bf16[96,192]{1,0:T(8,128)(2,1)S(1)} %copy-done.31), channel_id=1, replica_groups=mesh['dp'=8,'tensor'=4] {'dp'}, dimensions={0}, use_global_device_ids=true | all-gather | bytes 331776 | tf_op jit(solution)/shard_map/all_gather | solution.py:99
  201.6 98.7 %while.30 = (s32[]{:T(128)}, bf16[4,512,192]{1,2,0:T(8,128)(2,1)}, f32[4,3,512]{2,1,0:T(4,128)S(1)}, s32[4]{0:T(128)S(1)}, s32[1,2048]{1,0:T(1,128)S(1)}, /*inde...) while((s32[]{:T(128)}, bf16[4,512,192]{1,2,0:T(8,128)(2,1)}, ...), condition=%wide.region_5.6_spmd, body=%wide.region_2.5_spmd.sunk | while | flops 844200448 | bytes 44372400 | solution.py:172
  306.1 34.5 %reduce-scatter.19.cloned.1.call-done = bf16[512,768]{1,0:T(8,128)(2,1)} async-done(((bf16[2048,768]{1,0:T(8,128)(2,1)}), bf16[512,768]{1,0:T(8,128)(2,1)}) %reduce-scatter.19.cloned.1.call-update) | async-done | bytes 786448 | tf_op jit(solution)/shard_map/reduce_scatter | solution.py:175
  346.5 26.5 %all-gather = bf16[8,1,384]{2,1,0:T(2,128)(2,1)S(1)} all-gather(bf16[1,1,384]{2,1,0:T(2,128)(2,1)S(1)} %reshape.343), channel_id=1, replica_groups=mesh['dp'=8,'tensor'=4] {'dp'}, dimensions={0}, use_global_device_ids=true | all-gather | bytes 6912 | tf_op jit(solution)/shard_map/all_gather | solution.py:106
  375.9 7.6 fusion.139
  383.5 36.3 %all-gather.14.cloned.1.call-done = bf16[768,768]{0,1:T(8,128)(2,1)} async-done(((bf16[768,96]{0,1:T(8,128)(2,1)}), bf16[768,768]{0,1:T(8,128)(2,1)}) %all-gather.14.cloned.1.call-update) | async-done | bytes 1179664 | tf_op jit(solution)/shard_map/all_gather | solution.py:107
  419.8 28.5 %all-gather.16.cloned.1.call-done = bf16[2048,768]{1,0:T(8,128)(2,1)} async-done(((bf16[512,768]{1,0:T(8,128)(2,1)}), bf16[2048,768]{1,0:T(8,128)(2,1)}) %all-gather.16.cloned.1.call-update) | async-done | bytes 3145744 | tf_op jit(solution)/shard_map/all_gather | solution.py:200
  448.3 20.5 %fusion.132 = (bf16[768]{0:T(1024)(128)(2,1)}, bf16[2048,768]{1,0:T(8,128)(2,1)S(1)}, f32[2048,768]{1,0:T(8,128)}) fusion(f32[2048,768]{1,0:T(8,128)} %fusion.139, f32[768]{0:T(1024)S(1)} %dynamic-slice_convert_fusion, bf16[2048,768]{1,0:T(8,128)(2,1)} %all-gather.16.cloned.1.call-done, bf16[768,768]{0,1:T(8,128)(2,1)} %all-gather.14.cloned.1.call-done), kind=kOutput, calls=%fused_computation.174 | convolution fusion | flops 2532310272 | bytes 20058624 | tf_op jit(solution)/shard_map/dot_general | solution.py:45
  486.5 26.1 %reduce-scatter.23.cloned.1.call-done = bf16[512,768]{1,0:T(8,128)(2,1)} async-done(((bf16[2048,768]{1,0:T(8,128)(2,1)}), bf16[512,768]{1,0:T(8,128)(2,1)}) %reduce-scatter.23.cloned.1.call-update) | async-done | bytes 786448 | tf_op jit(solution)/shard_map/reduce_scatter | solution.py:208
  517.1 35.9 %reduce-scatter.21.cloned.1.call-done = bf16[512,768]{1,0:T(8,128)(2,1)} async-done(((bf16[2048,768]{1,0:T(8,128)(2,1)}), bf16[512,768]{1,0:T(8,128)(2,1)}) %reduce-scatter.21.cloned.1.call-update) | async-done | bytes 786448 | tf_op jit(solution)/shard_map/reduce_scatter | solution.py:184
  559.2 33.1 %all_gather.80 = bf16[768,192]{1,0:T(8,128)(2,1)} all-gather(bf16[96,192]{1,0:T(8,128)(2,1)S(1)} %copy-done.25), channel_id=1, replica_groups=mesh['dp'=8,'tensor'=4] {'dp'}, dimensions={0}, use_global_device_ids=true | all-gather | bytes 331776 | tf_op jit(solution)/shard_map/all_gather | solution.py:191
  603.3 258.0 %while.31 = (s32[]{:T(128)}, f32[1,2048,3,64]{1,3,2,0:T(8,128)}, f32[1,2048,3,64]{1,3,2,0:T(8,128)}, f32[4,512,3,64]{1,3,2,0:T(8,128)}, s32[4]{0:T(128)S(1)}, /*...) while((s32[]{:T(128)}, f32[1,2048,3,64]{1,3,2,0:T(8,128)}, ...), condition=%wide.region_15.16_spmd, body=%wide.region_13.15_spmd.sunk | while | flops 2096897024 | bytes 208079408 | solution.py:255
  624.7 20.9 %fusion.198 = f32[4,512,3,64]{1,3,2,0:T(8,128)} fusion(f32[4,512,3,64]{1,3,2,0:T(8,128)} %get-tuple-element.595, s32[]{:T(128)S(6)} %copy.90, f32[3,512,2048]{2,1,0:T(8,128)} %fusion.194, f32[3,512,2048]{2,1,0:T(8,128)} %copy-done, f32[3,512]{1,0:T(4,128)S(1)} %dynamic-slice_bitcast_fusion.2, pred[512,2048]{1,0:T(8,128)(4,1)S(1)} %broadcast_compare_fusion.5, ...), kind=kOutput, calls=%fused_computation.45.clone.1 | convolution fusion | flops 437259776 | bytes 53624836 | tf_op jit(solution)/shard_map/while/body/eval_jaxpr/hqk,khd->qhd/dot_general | solution.py:237
  645.7 22.6 %fusion.196 = f32[1,2048,3,64]{1,3,2,0:T(8,128)} fusion(f32[3,512,2048]{2,1,0:T(8,128)} %fusion.194, f32[3,512,2048]{2,1,0:T(8,128)} %copy-done, f32[3,512]{1,0:T(4,128)S(1)} %dynamic-slice_bitcast_fusion.2, pred[512,2048]{1,0:T(8,128)(4,1)S(1)} %broadcast_compare_fusion.5, f32[1,2048,3,64]{1,3,2,0:T(8,128)} %get-tuple-element.593, ...), kind=kOutput, calls=%fused_computation.40.clone.1 | convolution fusion | flops 437652992 | bytes 55787524 | tf_op jit(solution)/shard_map/while/body/eval_jaxpr/hqk,qhd->khd/dot_general | solution.py:238
  689.4 20.7 %fusion.198 = f32[4,512,3,64]{1,3,2,0:T(8,128)} fusion(f32[4,512,3,64]{1,3,2,0:T(8,128)} %get-tuple-element.595, s32[]{:T(128)S(6)} %copy.90, f32[3,512,2048]{2,1,0:T(8,128)} %fusion.194, f32[3,512,2048]{2,1,0:T(8,128)} %copy-done, f32[3,512]{1,0:T(4,128)S(1)} %dynamic-slice_bitcast_fusion.2, pred[512,2048]{1,0:T(8,128)(4,1)S(1)} %broadcast_compare_fusion.5, ...), kind=kOutput, calls=%fused_computation.45.clone.1 | convolution fusion | flops 437259776 | bytes 53624836 | tf_op jit(solution)/shard_map/while/body/eval_jaxpr/hqk,khd->qhd/dot_general | solution.py:237
  710.2 22.4 %fusion.196 = f32[1,2048,3,64]{1,3,2,0:T(8,128)} fusion(f32[3,512,2048]{2,1,0:T(8,128)} %fusion.194, f32[3,512,2048]{2,1,0:T(8,128)} %copy-done, f32[3,512]{1,0:T(4,128)S(1)} %dynamic-slice_bitcast_fusion.2, pred[512,2048]{1,0:T(8,128)(4,1)S(1)} %broadcast_compare_fusion.5, f32[1,2048,3,64]{1,3,2,0:T(8,128)} %get-tuple-element.593, ...), kind=kOutput, calls=%fused_computation.40.clone.1 | convolution fusion | flops 437652992 | bytes 55787524 | tf_op jit(solution)/shard_map/while/body/eval_jaxpr/hqk,qhd->khd/dot_general | solution.py:238
  753.7 20.7 %fusion.198 = f32[4,512,3,64]{1,3,2,0:T(8,128)} fusion(f32[4,512,3,64]{1,3,2,0:T(8,128)} %get-tuple-element.595, s32[]{:T(128)S(6)} %copy.90, f32[3,512,2048]{2,1,0:T(8,128)} %fusion.194, f32[3,512,2048]{2,1,0:T(8,128)} %copy-done, f32[3,512]{1,0:T(4,128)S(1)} %dynamic-slice_bitcast_fusion.2, pred[512,2048]{1,0:T(8,128)(4,1)S(1)} %broadcast_compare_fusion.5, ...), kind=kOutput, calls=%fused_computation.45.clone.1 | convolution fusion | flops 437259776 | bytes 53624836 | tf_op jit(solution)/shard_map/while/body/eval_jaxpr/hqk,khd->qhd/dot_general | solution.py:237
  774.5 22.4 %fusion.196 = f32[1,2048,3,64]{1,3,2,0:T(8,128)} fusion(f32[3,512,2048]{2,1,0:T(8,128)} %fusion.194, f32[3,512,2048]{2,1,0:T(8,128)} %copy-done, f32[3,512]{1,0:T(4,128)S(1)} %dynamic-slice_bitcast_fusion.2, pred[512,2048]{1,0:T(8,128)(4,1)S(1)} %broadcast_compare_fusion.5, f32[1,2048,3,64]{1,3,2,0:T(8,128)} %get-tuple-element.593, ...), kind=kOutput, calls=%fused_computation.40.clone.1 | convolution fusion | flops 437652992 | bytes 55787524 | tf_op jit(solution)/shard_map/while/body/eval_jaxpr/hqk,qhd->khd/dot_general | solution.py:238
  818.0 20.8 %fusion.198 = f32[4,512,3,64]{1,3,2,0:T(8,128)} fusion(f32[4,512,3,64]{1,3,2,0:T(8,128)} %get-tuple-element.595, s32[]{:T(128)S(6)} %copy.90, f32[3,512,2048]{2,1,0:T(8,128)} %fusion.194, f32[3,512,2048]{2,1,0:T(8,128)} %copy-done, f32[3,512]{1,0:T(4,128)S(1)} %dynamic-slice_bitcast_fusion.2, pred[512,2048]{1,0:T(8,128)(4,1)S(1)} %broadcast_compare_fusion.5, ...), kind=kOutput, calls=%fused_computation.45.clone.1 | convolution fusion | flops 437259776 | bytes 53624836 | tf_op jit(solution)/shard_map/while/body/eval_jaxpr/hqk,khd->qhd/dot_general | solution.py:237
  838.8 22.4 %fusion.196 = f32[1,2048,3,64]{1,3,2,0:T(8,128)} fusion(f32[3,512,2048]{2,1,0:T(8,128)} %fusion.194, f32[3,512,2048]{2,1,0:T(8,128)} %copy-done, f32[3,512]{1,0:T(4,128)S(1)} %dynamic-slice_bitcast_fusion.2, pred[512,2048]{1,0:T(8,128)(4,1)S(1)} %broadcast_compare_fusion.5, f32[1,2048,3,64]{1,3,2,0:T(8,128)} %get-tuple-element.593, ...), kind=kOutput, calls=%fused_computation.40.clone.1 | convolution fusion | flops 437652992 | bytes 55787524 | tf_op jit(solution)/shard_map/while/body/eval_jaxpr/hqk,qhd->khd/dot_general | solution.py:238
  878.9 7.6 fusion.114
  899.5 10.3 reduce-scatter.25.cloned.1.call-done
  914.9 10.3 all-reduce.19
  925.1 38.2 %all-reduce.17 = (f32[768]{0:T(1024)S(1)}, f32[768]{0:T(1024)S(1)}, f32[768]{0:T(1024)S(1)}, f32[768]{0:T(1024)S(1)}, f32[768]{0:T(1024)S(1)}, /*index=5*/f32[76...) all-reduce(bf16[768]{0:T(1024)(128)(2,1)S(1)} %get-tuple-element.37, ...), channel_id=6, replica_groups=mesh['dp'=8,'tensor'=4] {'dp'}, use_global_device_ids=true, to_apply=%region_21.22.clone | all-reduce | flops 9216 | bytes 55296
  970.3 13.2 %reduce-scatter.29.cloned.1.call-done = f32[768,96]{0,1:T(8,128)} async-done(((f32[768,768]{0,1:T(8,128)}), f32[768,96]{0,1:T(8,128)}) %reduce-scatter.29.cloned.1.call-update) | async-done | bytes 294928 | tf_op jit(solution)/shard_map/reduce_scatter | solution.py:316
  983.6 72.3 %reduce-scatter.27.cloned.1.call-done = f32[96,768]{1,0:T(8,128)} async-done(((f32[768,768]{1,0:T(8,128)}), f32[96,768]{1,0:T(8,128)}) %reduce-scatter.27.cloned.1.call-update) | async-done | bytes 294928 | tf_op jit(solution)/shard_map/reduce_scatter | solution.py:315
  1055.9 65.9 %reduce-scatter.35.cloned.1.call-done = f32[96,192]{1,0:T(8,128)} async-done(((f32[768,192]{1,0:T(8,128)}), f32[96,192]{1,0:T(8,128)}) %reduce-scatter.35.cloned.1.call-update) | async-done | bytes 73744
  1121.7 65.4 %reduce-scatter.33.cloned.1.call-done = f32[96,192]{1,0:T(8,128)} async-done(((f32[768,192]{1,0:T(8,128)}), f32[96,192]{1,0:T(8,128)}) %reduce-scatter.33.cloned.1.call-update) | async-done | bytes 73744
  1187.1 65.9 %reduce-scatter.31.cloned.1.call-done = f32[96,192]{1,0:T(8,128)} async-done(((f32[768,192]{1,0:T(8,128)}), f32[96,192]{1,0:T(8,128)}) %reduce-scatter.31.cloned.1.call-update) | async-done | bytes 73744
  (324 shorter events, 306.6 us)
Async XLA Ops:
  8.0 53.5 %copy-start.24 = (bf16[96,192]{1,0:T(8,128)(2,1)S(1)}, bf16[96,192]{1,0:T(8,128)(2,1)}, u32[]{:S(2)}) copy-start(bf16[96,192]{1,0:T(8,128)(2,1)} %param.29) | copy-start | bytes 110596
  8.0 53.6 %copy-start.32 = (bf16[192,96]{1,0:T(8,128)(2,1)S(1)}, bf16[192,96]{1,0:T(8,128)(2,1)}, u32[]{:S(2)}) copy-start(bf16[192,96]{1,0:T(8,128)(2,1)} %param.32) | copy-start | bytes 110596
  8.0 84.7 %copy-start.30 = (bf16[96,192]{1,0:T(8,128)(2,1)S(1)}, bf16[96,192]{1,0:T(8,128)(2,1)}, u32[]{:S(2)}) copy-start(bf16[96,192]{1,0:T(8,128)(2,1)} %param.27) | copy-start | bytes 110596
  8.1 116.1 %copy-start.31 = (bf16[96,192]{1,0:T(8,128)(2,1)S(1)}, bf16[96,192]{1,0:T(8,128)(2,1)}, u32[]{:S(2)}) copy-start(bf16[96,192]{1,0:T(8,128)(2,1)} %param.30) | copy-start | bytes 110596
  8.1 188.7 %all-gather.8.cloned.1.call-start = ((), (), s32[]{:S(2)}) async-start(), calls=%async_computation.10 | async-start | bytes 3932160 | tf_op jit(solution)/shard_map/all_gather | solution.py:125
  59.1 65.1 %copy-start.26 = (f32[768]{0:T(1024)}, f32[768]{0:T(1024)S(1)}, u32[]{:S(2)}) copy-start(f32[768]{0:T(1024)S(1)} %convert_element_type.172) | copy-start | bytes 9220
  61.5 279.1 %reduce-scatter.19.cloned.1.call-start = ((), (), s32[]{:S(2)}) async-start(), calls=%async_computation.11 | async-start | bytes 3932160 | tf_op jit(solution)/shard_map/reduce_scatter | solution.py:175
  61.6 93.7 %collective-permute-start = (bf16[96,192]{1,0:T(8,128)(2,1)S(1)}, bf16[96,192]{1,0:T(8,128)(2,1)S(1)}, u32[]{:S(2)}, u32[]{:S(2)}) collective-permute-start(bf16[96,192]{1,0:T(8,128)(2,1)S(1)} %copy-done.24), channel_id=1, source_target_pairs={{0,4},{4,8},{8,12},{12,16},{16,20},{20,24},{24,28},{28,0},{1,5},{5... | collective-permute-start | bytes 110600 | tf_op jit(solution)/shard_map/ppermute | solution.py:22
  92.8 209.1 %copy-start.13 = (bf16[192,768]{0,1:T(8,128)(2,1)}, bf16[192,768]{0,1:T(8,128)(2,1)S(1)}, u32[]{:S(2)}) copy-start(bf16[192,768]{0,1:T(8,128)(2,1)S(1)} %all_gather.69) | copy-start | bytes 884740
  124.2 72.6 %copy-start.19 = (bf16[768,192]{1,0:T(8,128)(2,1)}, bf16[768,192]{1,0:T(8,128)(2,1)S(1)}, u32[]{:S(2)}) copy-start(bf16[768,192]{1,0:T(8,128)(2,1)S(1)} %all_gather.65) | copy-start | bytes 884740
  155.2 6.8 collective-permute-start.1
  162.1 6.8 collective-permute-start.2
  168.8 6.8 collective-permute-start.3
  175.6 6.8 collective-permute-start.4
  182.4 6.8 collective-permute-start.5
  189.2 7.0 collective-permute-start.6
  305.5 67.7 %all-gather.12.cloned.1.call-start = ((), (), s32[]{:S(2)}) async-start(), calls=%async_computation.13 | async-start | bytes 1327104 | tf_op jit(solution)/shard_map/all_gather | solution.py:105
  306.0 69.9 %all-gather.10.cloned.1.call-start = ((), (), s32[]{:S(2)}) async-start(), calls=%async_computation.12 | async-start | bytes 3932160 | tf_op jit(solution)/shard_map/all_gather | solution.py:180
  345.1 74.6 %all-gather.14.cloned.1.call-start = ((), (), s32[]{:S(2)}) async-start(), calls=%async_computation.14 | async-start | bytes 1327104 | tf_op jit(solution)/shard_map/all_gather | solution.py:107
  345.7 102.6 %all-gather.16.cloned.1.call-start = ((), (), s32[]{:S(2)}) async-start(), calls=%async_computation.16 | async-start | bytes 3932160 | tf_op jit(solution)/shard_map/all_gather | solution.py:200
  346.5 166.1 %reduce-scatter.23.cloned.1.call-start = ((), (), s32[]{:S(2)}) async-start(), calls=%async_computation.17 | async-start | bytes 3932160 | tf_op jit(solution)/shard_map/reduce_scatter | solution.py:208
  474.5 78.5 %reduce-scatter.21.cloned.1.call-start = ((), (), s32[]{:S(2)}) async-start(), calls=%async_computation.15 | async-start | bytes 3932160 | tf_op jit(solution)/shard_map/reduce_scatter | solution.py:184
  485.8 106.5 %all-gather.18.cloned.1.call-start = ((), (), s32[]{:S(2)}) async-start(), calls=%async_computation.18 | async-start | bytes 3932160 | tf_op jit(solution)/shard_map/all_gather | solution.py:219
  559.1 338.7 %reduce-scatter.37.cloned.1.call-start = ((), (), s32[]{:S(2)}) async-start(), calls=%async_computation.25 | async-start | bytes 884736
  596.5 313.2 %reduce-scatter.25.cloned.1.call-start = ((), (), s32[]{:S(2)}) async-start(), calls=%async_computation.19 | async-start | bytes 3932160 | tf_op jit(solution)/shard_map/reduce_scatter | solution.py:268
  871.8 111.8 %reduce-scatter.29.cloned.1.call-start = ((), (), s32[]{:S(2)}) async-start(), calls=%async_computation.21 | async-start | bytes 2654208 | tf_op jit(solution)/shard_map/reduce_scatter | solution.py:316
  878.8 177.0 %reduce-scatter.27.cloned.1.call-start = ((), (), s32[]{:S(2)}) async-start(), calls=%async_computation.20 | async-start | bytes 2654208 | tf_op jit(solution)/shard_map/reduce_scatter | solution.py:315
  886.6 235.2 %reduce-scatter.35.cloned.1.call-start = ((), (), s32[]{:S(2)}) async-start(), calls=%async_computation.24 | async-start | bytes 884736
  891.8 295.3 %reduce-scatter.33.cloned.1.call-start = ((), (), s32[]{:S(2)}) async-start(), calls=%async_computation.23 | async-start | bytes 884736
  893.1 359.9 %reduce-scatter.31.cloned.1.call-start = ((), (), s32[]{:S(2)}) async-start(), calls=%async_computation.22 | async-start | bytes 884736
  896.2 72.4 %copy-start.5 = (f32[512,768]{1,0:T(8,128)S(1)}, f32[512,768]{1,0:T(8,128)}, u32[]{:S(2)}) copy-start(f32[512,768]{1,0:T(8,128)} %copy-done.4) | copy-start | bytes 4718596
  909.7 58.9 %copy-start.7 = (bf16[512,768]{1,0:T(8,128)(2,1)S(1)}, bf16[512,768]{1,0:T(8,128)(2,1)}, u32[]{:S(2)}) copy-start(bf16[512,768]{1,0:T(8,128)(2,1)} %reduce-scatter.25.cloned.1.call-done) | copy-start | bytes 2359300
  (42 other events, 520.6 us)
Sparse Core Ops, SparseCore 0:
  61.6 25.7 all-gather.7
  305.6 34.9 reduce-scatter.18
  474.6 37.9 reduce-scatter.22
  514.9 37.9 reduce-scatter.20
Sparse Core Ops, SparseCore 1:
  308.4 38.5 all-gather.11
  349.0 26.8 all-gather.9
  378.2 41.5 all-gather.13
  421.4 26.8 all-gather.15
  559.2 28.3 all-gather.17
  596.6 62.6 reduce-scatter.36
  871.9 37.8 reduce-scatter.24
  914.1 69.4 reduce-scatter.28
  987.9 67.9 reduce-scatter.26
  1060.1 61.6 reduce-scatter.34
  1125.5 61.6 reduce-scatter.32
  1191.4 61.6 reduce-scatter.30
